TPU v7x, 32 devices: a whole 2x2x4 slice. The times are simulated.
32 devices in a mesh: grp: 4 (over z), shard: 8 (over y, x, core).
Axes of the slice: x: 2, y: 2, z: 4, core: 2. Of those that a mesh axis runs over, the one named last changes fastest.
Arguments:
- table: float32 [1024, 8, 128], P('shard')
- table_first: float32 [1024, 8, 128], P('shard'), may hold values from -3 to 3
- table_second: float32 [1024, 8, 128], P('shard')
- slot_table: int32 [1024], P('shard'), may hold values from 0 to 25
- touched: int32 [4, 256], P('grp', 'shard'), may hold values from 0 to 1023, as said below
- emb_grads: bfloat16 [4, 256, 8, 128], P('grp', 'shard'), may hold values from -6 to 6
- block_slot: int32 [1024], replicated, may hold values from 0 to 1023, as said below
- dense_x: bfloat16 [13, 131072], P(None, ('grp', 'shard')), may hold values from -6 to 6
- dense_cot: bfloat16 [131072, 128], P(('grp', 'shard')), may hold values from -0.15625 to 0.15625
- w_one: float32 [13, 512], replicated, may hold values from -1.75 to 1.75
- w_two: float32 [512, 256], replicated, may hold values from -0.25 to 0.25
- w_three: float32 [256, 128], replicated, may hold values from -0.375 to 0.375
- first_one: float32 [13, 512], replicated, may hold values from -3 to 3
- first_two: float32 [512, 256], replicated, may hold values from -3 to 3
- first_three: float32 [256, 128], replicated, may hold values from -3 to 3
- second_one: float32 [13, 512], replicated, may hold values from 0.001 to 0.3
- second_two: float32 [512, 256], replicated, may hold values from 0.001 to 0.3
- second_three: float32 [256, 128], replicated, may hold values from 0.001 to 0.3
Outputs:
- new_table: float32 [1024, 8, 128], P('shard')
- new_table_first: float32 [1024, 8, 128], P('shard')
- new_table_second: float32 [1024, 8, 128], P('shard')
- new_w_one: float32 [13, 512], replicated
- new_w_two: float32 [512, 256], replicated
- new_w_three: float32 [256, 128], replicated
- new_first_one: float32 [13, 512], replicated
- new_first_two: float32 [512, 256], replicated
- new_first_three: float32 [256, 128], replicated
- new_second_one: float32 [13, 512], replicated
- new_second_two: float32 [512, 256], replicated
- new_second_three: float32 [256, 128], replicated
Inputs may be any that keep to these rules, and one draw needn't show every extreme that they name: `touched`: each device's 32 ids are distinct; at most 8 of them have block_slot // 128 equal to any one shard, and in every draw some shard gets exactly 8 from every device. `block_slot`: A permutation of the 1024 slots.
All inputs are finite; a program needn't handle non-finite values.
Results may differ from a plain program's by a relative error of at most 0.0037.
Values may be sent and summed in bfloat16 or wider, within the bound.
A program may use at most 128 MiB of HBM per device.

v0:
```python
import jax
import jax.numpy as jnp
from jax import lax
from jax.sharding import PartitionSpec as P

TABLES = 26
CAP = 8


beta_one = 0.9
beta_two = 0.999
corr_first = 1.0 - 0.9**10
corr_second = 1.0 - 0.999**10
adam_eps = 1e-06
decay_rate = 0.01
learn_rate = 0.1
ratio_eps = 1e-06


def silu_slope(pre_value):
    logistic = jax.nn.sigmoid(pre_value)
    return logistic * (1.0 + pre_value * (1.0 - logistic))


def tower_grads(dense_x, dense_cot, w_one, w_two, w_three):
    w_one_bf = w_one.astype(jnp.bfloat16)
    w_two_bf = w_two.astype(jnp.bfloat16)
    w_three_bf = w_three.astype(jnp.bfloat16)
    pre_one = lax.dot_general(
        dense_x, w_one_bf, (((0,), (0,)), ((), ())), preferred_element_type=jnp.float32
    )
    hidden_one = jax.nn.silu(pre_one).astype(jnp.bfloat16)
    pre_two = jnp.dot(hidden_one, w_two_bf, preferred_element_type=jnp.float32)
    hidden_two = jax.nn.silu(pre_two).astype(jnp.bfloat16)
    grad_three = lax.dot_general(
        hidden_two, dense_cot, (((0,), (0,)), ((), ())), preferred_element_type=jnp.float32
    )
    back_two = (
        lax.dot_general(
            dense_cot, w_three_bf, (((1,), (1,)), ((), ())), preferred_element_type=jnp.float32
        )
        * silu_slope(pre_two)
    ).astype(jnp.bfloat16)
    grad_two = lax.dot_general(
        hidden_one, back_two, (((0,), (0,)), ((), ())), preferred_element_type=jnp.float32
    )
    back_one = (
        lax.dot_general(
            back_two, w_two_bf, (((1,), (1,)), ((), ())), preferred_element_type=jnp.float32
        )
        * silu_slope(pre_one)
    ).astype(jnp.bfloat16)
    grad_one = jnp.dot(dense_x, back_one, preferred_element_type=jnp.float32)
    return (grad_one, grad_two, grad_three)


def lamb_dense(weight, first_in, second_in, gradient):
    first_out = beta_one * first_in + (1.0 - beta_one) * gradient
    second_out = beta_two * second_in + (1.0 - beta_two) * gradient * gradient
    update = (
        first_out / corr_first / (jnp.sqrt(second_out / corr_second) + adam_eps)
        + decay_rate * weight
    )
    trust_ratio = jnp.sqrt(jnp.sum(weight * weight)) / (
        jnp.sqrt(jnp.sum(update * update)) + ratio_eps
    )
    return (weight - learn_rate * trust_ratio * update, first_out, second_out)


def body(
    table,
    table_first,
    table_second,
    slot_table,
    touched,
    emb_grads,
    block_slot,
    dense_x,
    dense_cot,
    w_one,
    w_two,
    w_three,
    first_one,
    first_two,
    first_three,
    second_one,
    second_two,
    second_three,
):
    shards = lax.axis_size("shard")
    local_blocks = table.shape[0]
    block_rows = table.shape[1]
    emb_width = table.shape[2]
    row_width = block_rows * emb_width
    capacity = CAP
    dense_terms = tower_grads(dense_x, dense_cot, w_one, w_two, w_three)
    table_hot = (slot_table[:, None] == jnp.arange(TABLES, dtype=jnp.int32)[None, :]).astype(
        jnp.float32
    )
    row_weight = jnp.sum(table * table, axis=(1, 2))
    part_weight = jnp.dot(row_weight, table_hot, precision=lax.Precision.HIGHEST)
    block_ids = touched[0]
    count_touched = block_ids.shape[0]
    grad_rows = emb_grads[0].reshape(count_touched, row_width)
    slot_index = jnp.take(block_slot, block_ids)
    owner_shard = slot_index // local_blocks
    local_row = slot_index % local_blocks
    owner_hot = (owner_shard[:, None] == jnp.arange(shards, dtype=jnp.int32)[None, :]).astype(
        jnp.int32
    )
    bucket_rank = jnp.cumsum(owner_hot, axis=0) - 1
    bucket_place = jnp.sum(owner_hot * bucket_rank, axis=1)
    send_index = owner_shard * capacity + bucket_place
    picker = jnp.arange(shards * capacity, dtype=jnp.int32)[:, None] == send_index[None, :]
    send_rows = jnp.dot(
        picker.astype(jnp.bfloat16), grad_rows, preferred_element_type=jnp.float32
    ).astype(jnp.bfloat16)
    send_local = jnp.where(
        jnp.any(picker, axis=1), jnp.sum(jnp.where(picker, local_row[None, :], 0), axis=1), -1
    )
    send_rows = send_rows.reshape(shards, capacity, row_width)
    send_local = send_local.reshape(shards, capacity)
    recv_rows, recv_local = (
        lax.all_to_all(send_rows, "shard", split_axis=0, concat_axis=0, tiled=True),
        lax.all_to_all(send_local, "shard", split_axis=0, concat_axis=0, tiled=True),
    )
    piece_rows = lax.all_gather(recv_rows, "grp", axis=0, tiled=True).reshape(-1, row_width)
    piece_locals = lax.all_gather(recv_local, "grp", axis=0, tiled=True).reshape(-1)
    matches = piece_locals[:, None] == jnp.arange(local_blocks, dtype=jnp.int32)[None, :]
    summed = lax.dot_general(
        matches.astype(jnp.bfloat16),
        piece_rows,
        (((0,), (0,)), ((), ())),
        preferred_element_type=jnp.float32,
    )
    counted = jnp.sum(matches.astype(jnp.float32), axis=0)
    emb_grad = summed.reshape(local_blocks, block_rows, emb_width)
    touched_mask = (counted > 0.5)[:, None, None]
    new_first = jnp.where(
        touched_mask, beta_one * table_first + (1.0 - beta_one) * emb_grad, table_first
    )
    new_second = jnp.where(
        touched_mask, beta_two * table_second + (1.0 - beta_two) * emb_grad * emb_grad, table_second
    )
    update = jnp.where(
        touched_mask,
        new_first / corr_first / (jnp.sqrt(new_second / corr_second) + adam_eps)
        + decay_rate * table,
        0.0,
    )
    row_update = jnp.sum(update * update, axis=(1, 2))
    part_update = jnp.dot(row_update, table_hot, precision=lax.Precision.HIGHEST)
    dense_grads = lax.psum((dense_terms[0], dense_terms[1], dense_terms[2]), ("grp", "shard"))
    weight_total, update_total = lax.psum((part_weight, part_update), "shard")
    table_ratio = jnp.sqrt(weight_total) / (jnp.sqrt(update_total) + ratio_eps)
    ratio_rows = jnp.dot(table_hot, table_ratio, precision=lax.Precision.HIGHEST)
    new_table = table - learn_rate * ratio_rows[:, None, None] * update
    layer_one = lamb_dense(w_one, first_one, second_one, dense_grads[0])
    layer_two = lamb_dense(w_two, first_two, second_two, dense_grads[1])
    layer_three = lamb_dense(w_three, first_three, second_three, dense_grads[2])
    return (
        new_table,
        new_first,
        new_second,
        layer_one[0],
        layer_two[0],
        layer_three[0],
        layer_one[1],
        layer_two[1],
        layer_three[1],
        layer_one[2],
        layer_two[2],
        layer_three[2],
    )


def solution(mesh):
    return jax.shard_map(
        body,
        mesh=mesh,
        in_specs=(
            P("shard", None, None),
            P("shard", None, None),
            P("shard", None, None),
            P("shard"),
            P("grp", "shard"),
            P("grp", "shard", None, None),
            P(),
            P(None, ("grp", "shard")),
            P(("grp", "shard"), None),
            P(),
            P(),
            P(),
            P(),
            P(),
            P(),
            P(),
            P(),
            P(),
        ),
        out_specs=(
            P("shard", None, None),
            P("shard", None, None),
            P("shard", None, None),
            P(),
            P(),
            P(),
            P(),
            P(),
            P(),
            P(),
            P(),
            P(),
        ),
        check_vma=False,
    )
```

profile of v0, /device:TPU:0, one launch (start us, length us, event | category | flops | bytes accessed | tf_op | source)
XLA Modules:
  0.0 179.8 jit_solution(11988659728228566340)
XLA Ops:
  7.9 1.4 gather_fusion
  11.9 5.2 %all-to-all-start = ((s32[8,1,8]{2,1,0:T(1,128)}), s32[8,1,8]{2,1,0:T(1,128)S(1)}, u32[]{:S(2)}, u32[]{:S(2)}) async-start(s32[8,1,8]{2,1,0:T(1,128)} %bitcast.9), calls=%async_computation | async-start | bytes 8192 | tf_op jit(solution)/shard_map/all_to_all | solution.py:125
  17.1 6.6 %multiply_convert_fusion.1 = (bf16[4096,512]{1,0:T(8,128)(2,1)S(1)}, f32[4096,512]{1,0:T(8,128)}) fusion(bf16[13,4096]{1,0:T(8,128)(2,1)} %param.25, f32[13,512]{1,0:T(8,128)} %param.27), kind=kOutput, calls=%fused_computation.2 | convolution fusion | flops 65018368 | bytes 12716032 | tf_op jit(solution)/shard_map/dot_general | solution.py:29
  23.7 1.3 fusion.12
  25.0 2.0 %fusion.1 = f32[256,128]{1,0:T(8,128)} fusion(bf16[4096,128]{1,0:T(8,128)(2,1)S(1)} %copy-done, f32[4096,256]{1,0:T(8,128)S(1)} %fusion.12), kind=kOutput, calls=%fused_computation.8 | convolution fusion | flops 273678336 | bytes 5373952 | tf_op jit(solution)/shard_map/dot_general | solution.py:35
  26.9 1.7 fusion
  28.7 1.4 copy-done.19
  30.1 2.1 %fusion.46 = f32[512,256]{1,0:T(8,128)} fusion(bf16[4096,512]{1,0:T(8,128)(2,1)S(1)} %get-tuple-element.94, bf16[4096,256]{1,0:T(8,128)(2,1)S(1)} %fusion), kind=kOutput, calls=%fused_computation.101 | convolution fusion | flops 1073741824 | bytes 6815744 | tf_op jit(solution)/shard_map/dot_general | solution.py:44
  32.4 1.0 multiply_reduce_fusion.3
  34.5 7.7 %fusion.4 = f32[13,512]{1,0:T(8,128)S(1)} fusion(bf16[13,4096]{1,0:T(8,128)(2,1)} %param.25, f32[4096,512]{1,0:T(8,128)} %get-tuple-element.95, bf16[4096,256]{1,0:T(8,128)(2,1)} %copy-done.19, f32[512,256]{1,0:T(8,128)S(1)} %copy-done.1), kind=kOutput, calls=%fused_computation.12 | convolution fusion | flops 1147273216 | bytes 11143168 | tf_op jit(solution)/shard_map/dot_general | solution.py:53
  42.1 41.0 %psum.37 = f32[13,512]{1,0:T(8,128)S(1)} all-reduce(f32[13,512]{1,0:T(8,128)S(1)} %fusion.4), channel_id=1, replica_groups=mesh['grp'=4,'shard'=8] {'grp','shard'}, use_global_device_ids=true, to_apply=%region_10.11 | all-reduce | flops 6656 | bytes 53248 | tf_op jit(solution)/shard_map/psum | solution.py:153
  86.2 1.0 copy.73
  87.4 3.6 %all-to-all-start.1 = ((bf16[8,8,1024]{2,1,0:T(8,128)(2,1)}), bf16[8,8,1024]{2,1,0:T(8,128)(2,1)S(1)}, u32[]{:S(2)}, u32[]{:S(2)}) async-start(bf16[8,8,1024]{2,1,0:T(8,128)(2,1)} %fusion.3), calls=%async_computation.1 | async-start | bytes 262144 | tf_op jit(solution)/shard_map/all_to_all | solution.py:124
  91.0 13.2 %all-gather = s32[32,1,8]{2,1,0:T(1,128)S(1)} all-gather(s32[8,1,8]{2,1,0:T(1,128)S(1)} %all-to-all-done), channel_id=2, replica_groups=mesh['grp'=4,'shard'=8] {'grp'}, dimensions={0}, use_global_device_ids=true | all-gather | bytes 1280 | tf_op jit(solution)/shard_map/all_gather | solution.py:128
  105.7 16.0 %all_gather.7 = bf16[32,8,1024]{2,1,0:T(8,128)(2,1)S(1)} all-gather(bf16[8,8,1024]{2,1,0:T(8,128)(2,1)S(1)} %all-to-all-done.1), channel_id=1, replica_groups=mesh['grp'=4,'shard'=8] {'grp'}, dimensions={0}, use_global_device_ids=true | all-gather | bytes 655360 | tf_op jit(solution)/shard_map/all_gather | solution.py:127
  121.7 1.0 copy.74
  122.7 2.9 %multiply_reduce_fusion.2 = (f32[128]{0:T(128)S(1)}, f32[128,8,128]{0,2,1:T(8,128)}, f32[128,8,128]{0,2,1:T(8,128)}, f32[128,8,128]{0,2,1:T(8,128)S(1)}) fusion(f32[128,8,128]{0,2,1:T(8,128)S(1)} %copy.79, pred[128]{0:T(512)(128)(4,1)S(1)} %broadcast_compare_fusion, f32[128,8,128]{0,2,1:T(8,128)} %copy.73, f32[128,8,128]{0,2,1:T(8,128)S(1)} %copy.76, ...), kind=kOutput, calls=%fused_computation.28 | convolution fusion | flops 69500800 | bytes 3671680 | tf_op jit(solution)/shard_map/dot_general | solution.py:130
  125.8 11.8 %all-reduce.1 = (f32[26]{0:T(128)S(1)}, f32[26]{0:T(128)S(1)}) all-reduce(f32[26]{0:T(128)S(1)} %convolution_bitcast_fusion.1, f32[26]{0:T(128)S(1)} %convolution_bitcast_fusion.2), channel_id=1, replica_groups=mesh['grp'=4,'shard'=8] {'shard'}, use_global_device_ids=true, to_apply=%region_8.9 | all-reduce | flops 52 | bytes 416 | tf_op jit(solution)/shard_map/psum | solution.py:154
  137.8 1.1 multiply_subtract_fusion.1
  139.9 2.0 %copy.81 = f32[128,8,128]{2,1,0:T(8,128)} copy(f32[128,8,128]{0,2,1:T(8,128)} %get-tuple-element.90) | data formatting | bytes 1048576
  143.0 21.3 %all-reduce.4.cloned.1.call-done = (f32[512,256]{1,0:T(8,128)}, f32[256,128]{1,0:T(8,128)}) async-done(((f32[512,256]{1,0:T(8,128)}, f32[256,128]{1,0:T(8,128)}), (f32[512,256]{1,0:T(8,128)}, f32[256,128]{1,0:T(8,128)})) %all-reduce.4.cloned.1.call-update) | async-done | bytes 655376 | tf_op jit(solution)/shard_map/psum | solution.py:153
  164.2 2.4 %multiply_reduce_fusion = (f32[]{:T(128)}, f32[]{:T(128)}, f32[512,256]{1,0:T(8,128)S(1)}, f32[512,256]{1,0:T(8,128)S(1)}) fusion(f32[512,256]{1,0:T(8,128)S(1)} %copy-done.1, f32[512,256]{1,0:T(8,128)} %get-tuple-element.78, f32[512,256]{1,0:T(8,128)} %param.31, f32[512,256]{1,0:T(8,128)} %param.34), kind=kLoop, calls=%fused_computation.23 | loop fusion | flops 2228222 | bytes 3145736 | tf_op jit(solution)/shard_map/reduce_sum | solution.py:65
  168.1 1.6 multiply_reduce_fusion.4
  171.1 1.1 multiply_subtract_fusion
  (71 shorter events, 10.9 us)
Async XLA Ops:
  7.2 17.8 %copy-start = (bf16[4096,128]{1,0:T(8,128)(2,1)S(1)}, bf16[4096,128]{1,0:T(8,128)(2,1)}, u32[]{:S(2)}) copy-start(bf16[4096,128]{1,0:T(8,128)(2,1)} %param.26) | copy-start | bytes 3145732
  11.9 75.5 %all-to-all-start = ((s32[8,1,8]{2,1,0:T(1,128)}), s32[8,1,8]{2,1,0:T(1,128)S(1)}, u32[]{:S(2)}, u32[]{:S(2)}) async-start(s32[8,1,8]{2,1,0:T(1,128)} %bitcast.9), calls=%async_computation | async-start | bytes 8192 | tf_op jit(solution)/shard_map/all_to_all | solution.py:125
  17.1 6.6 %copy-start.1 = (f32[512,256]{1,0:T(8,128)S(1)}, f32[512,256]{1,0:T(8,128)}, u32[]{:S(2)}) copy-start(f32[512,256]{1,0:T(8,128)} %param.28) | copy-start | bytes 1572868
  17.1 147.2 %all-reduce.4.cloned.1.call-start = ((), (), s32[]{:S(2)}) async-start(), calls=%async_computation.2 | async-start | bytes 1310720 | tf_op jit(solution)/shard_map/psum | solution.py:153
  25.0 2.0 %copy-start.7 = (f32[256,128]{1,0:T(8,128)S(1)}, f32[256,128]{1,0:T(8,128)}, u32[]{:S(2)}) copy-start(f32[256,128]{1,0:T(8,128)} %param.29) | copy-start | bytes 393220
  28.7 1.4 copy-start.19
  30.1 2.1 %copy-start.2 = (f32[128,8,128]{2,1,0:T(8,128)S(1)}, f32[128,8,128]{2,1,0:T(8,128)}, u32[]{:S(2)}) copy-start(f32[128,8,128]{2,1,0:T(8,128)} %param.18) | copy-start | bytes 1572868
  30.1 3.4 %copy-start.15 = (bf16[1,32,8,128]{3,2,1,0:T(8,128)(2,1)S(1)}, bf16[1,32,8,128]{3,2,1,0:T(8,128)(2,1)}, u32[]{:S(2)}) copy-start(bf16[1,32,8,128]{3,2,1,0:T(8,128)(2,1)} %param.23) | copy-start | bytes 196612
  34.4 48.7 %copy-start.12 = (f32[13,512]{1,0:T(8,128)S(1)}, f32[13,512]{1,0:T(8,128)}, u32[]{:S(2)}) copy-start(f32[13,512]{1,0:T(8,128)} %param.27) | copy-start | bytes 79876
  34.4 48.7 %copy-start.16 = (f32[13,512]{1,0:T(8,128)S(1)}, f32[13,512]{1,0:T(8,128)}, u32[]{:S(2)}) copy-start(f32[13,512]{1,0:T(8,128)} %param.30) | copy-start | bytes 79876
  34.4 48.8 %copy-start.17 = (f32[13,512]{1,0:T(8,128)S(1)}, f32[13,512]{1,0:T(8,128)}, u32[]{:S(2)}) copy-start(f32[13,512]{1,0:T(8,128)} %param.33) | copy-start | bytes 79876
  34.4 50.8 %copy-start.18 = (s32[128]{0:T(128)S(1)}, s32[128]{0:T(128)}, u32[]{:S(2)}) copy-start(s32[128]{0:T(128)} %param.21) | copy-start | bytes 1540
  34.4 51.7 %copy-start.5 = (f32[128,8,128]{2,1,0:T(8,128)S(1)}, f32[128,8,128]{2,1,0:T(8,128)}, u32[]{:S(2)}) copy-start(f32[128,8,128]{2,1,0:T(8,128)} %param.19) | copy-start | bytes 1572868
  34.4 52.7 %copy-start.6 = (f32[128,8,128]{2,1,0:T(8,128)S(1)}, f32[128,8,128]{2,1,0:T(8,128)}, u32[]{:S(2)}) copy-start(f32[128,8,128]{2,1,0:T(8,128)} %param.20) | copy-start | bytes 1572868
  83.8 21.8 %copy-start.13 = (f32[13,512]{1,0:T(8,128)}, f32[13,512]{1,0:T(8,128)S(1)}, u32[]{:S(2)}) copy-start(f32[13,512]{1,0:T(8,128)S(1)} %get-tuple-element.86) | copy-start | bytes 79876
  83.8 21.8 %copy-start.14 = (f32[13,512]{1,0:T(8,128)}, f32[13,512]{1,0:T(8,128)S(1)}, u32[]{:S(2)}) copy-start(f32[13,512]{1,0:T(8,128)S(1)} %get-tuple-element.87) | copy-start | bytes 79876
  87.4 18.2 %all-to-all-start.1 = ((bf16[8,8,1024]{2,1,0:T(8,128)(2,1)}), bf16[8,8,1024]{2,1,0:T(8,128)(2,1)S(1)}, u32[]{:S(2)}, u32[]{:S(2)}) async-start(bf16[8,8,1024]{2,1,0:T(8,128)(2,1)} %fusion.3), calls=%async_computation.1 | async-start | bytes 262144 | tf_op jit(solution)/shard_map/all_to_all | solution.py:124
  125.6 42.5 %copy-start.10 = (f32[256,128]{1,0:T(8,128)S(1)}, f32[256,128]{1,0:T(8,128)}, u32[]{:S(2)}) copy-start(f32[256,128]{1,0:T(8,128)} %param.32) | copy-start | bytes 393220
  125.6 42.5 %copy-start.11 = (f32[256,128]{1,0:T(8,128)S(1)}, f32[256,128]{1,0:T(8,128)}, u32[]{:S(2)}) copy-start(f32[256,128]{1,0:T(8,128)} %param.35) | copy-start | bytes 393220
  166.6 6.3 %copy-start.3 = (f32[512,256]{1,0:T(8,128)}, f32[512,256]{1,0:T(8,128)S(1)}, u32[]{:S(2)}) copy-start(f32[512,256]{1,0:T(8,128)S(1)} %get-tuple-element.84) | copy-start | bytes 1572868
  166.6 6.3 %copy-start.4 = (f32[512,256]{1,0:T(8,128)}, f32[512,256]{1,0:T(8,128)S(1)}, u32[]{:S(2)}) copy-start(f32[512,256]{1,0:T(8,128)S(1)} %get-tuple-element.85) | copy-start | bytes 1572868
  169.7 3.2 %copy-start.8 = (f32[256,128]{1,0:T(8,128)}, f32[256,128]{1,0:T(8,128)S(1)}, u32[]{:S(2)}) copy-start(f32[256,128]{1,0:T(8,128)S(1)} %get-tuple-element.82) | copy-start | bytes 393220
  169.7 3.2 %copy-start.9 = (f32[256,128]{1,0:T(8,128)}, f32[256,128]{1,0:T(8,128)S(1)}, u32[]{:S(2)}) copy-start(f32[256,128]{1,0:T(8,128)S(1)} %get-tuple-element.83) | copy-start | bytes 393220
Sparse Core Ops, SparseCore 0:
  32.3 131.8 all-reduce.3
where the time goes:
time: 180 us
  blocking collectives  82 us (46%)
  matrix products  25.8 us (14%)
  waiting for transfers between devices  21.3 us (12%)
  between operations  18.6 us (10%)
  other arithmetic  12.7 us (7%)
  local copies, waits for them, and re-layouts  10.6 us (6%)
  starting transfers between devices  8.81 us (5%)
    psum x1, blocking collectives, body(): lax.psum((dense_terms[0], dense_terms[1], dense_terms[2]), ('grp', 'shard'))  41 us
    psum x1, waiting for transfers between devices, body(): lax.psum((dense_terms[0], dense_terms[1], dense_terms[2]), ('grp', 'shard'))  21.3 us
    all_gather x1, blocking collectives, body(): lax.all_gather(recv_rows, 'grp', axis=0, tiled=True).reshape(-1, row_width)  16 us
    all_gather x1, blocking collectives, body(): lax.all_gather(recv_local, 'grp', axis=0, tiled=True).reshape(-1)  13.2 us
    psum x1, blocking collectives, body(): weight_total, update_total = lax.psum((part_weight, part_update), 'shard')  11.8 us
    dot_general x1, matrix products, tower_grads(): grad_one = jnp.dot(dense_x, back_one, preferred_element_type=jnp.float32)  7.68 us
    unnamed x46, local copies, waits for them, and re-layouts  6.98 us
    dot_general x1, matrix products, tower_grads(): lax.dot_general(dense_x, w_one_bf, (((0,), (0,)), ((), ())), preferred_el...  6.56 us
  transfers between devices with their start and end apart: 3, of which 1 were waited for; matrix products, arithmetic and copies ran while one was open for 21% of the time, Pallas kernels for 0%

commit v1 on v0

v1 whole, which is shorter than its diff:
```python
import functools
import jax
import jax.numpy as jnp
from jax import lax
from jax.experimental import pallas as pl
from jax.experimental.pallas import tpu as pltpu
from jax.sharding import PartitionSpec as P

TABLES = 26
CAP = 8

beta_one = 0.9
beta_two = 0.999
corr_first = 1.0 - 0.9**10
corr_second = 1.0 - 0.999**10
adam_eps = 1e-06
decay_rate = 0.01
learn_rate = 0.1
ratio_eps = 1e-06

MESH = pl.DeviceIdType.MESH
F32 = jnp.float32
BF16 = jnp.bfloat16
NN = (((1,), (0,)), ((), ()))
NT = (((1,), (1,)), ((), ()))
TN = (((0,), (0,)), ((), ()))


def mm(a, b, dims=NN):
    return lax.dot_general(a, b, dims, preferred_element_type=F32)


def iota(shape, axis):
    return lax.broadcasted_iota(jnp.int32, shape, axis).astype(F32)


def to_col(row, eye):
    return jnp.sum(jnp.where(eye, row, 0.0), axis=1, keepdims=True)


def to_row(col, eye):
    return jnp.sum(jnp.where(eye, col, 0.0), axis=0, keepdims=True)


def square_eye(count):
    return iota((count, count), 0) == iota((count, count), 1)


def gate(pre):
    logistic = 0.5 * jnp.tanh(0.5 * pre) + 0.5
    hidden = pre * logistic
    return hidden, logistic + hidden * (1.0 - logistic)


def adam(first_in, second_in, gradient, weight):
    first_out = beta_one * first_in + (1.0 - beta_one) * gradient
    second_out = beta_two * second_in + (1.0 - beta_two) * gradient * gradient
    update = (
        first_out / corr_first / (jnp.sqrt(second_out / corr_second) + adam_eps)
        + decay_rate * weight
    )
    return first_out, second_out, update


def exchange_kernel(
    grps,
    shards,
    chunk,
    touched,
    block_slot,
    slot_table,
    emb_grads,
    x,
    cot,
    w_one,
    w_two,
    w_three,
    table,
    table_first,
    table_second,
    emb_out,
    rate_out,
    g_one,
    g_two,
    g_three,
    w1t,
    w2t,
    w2b,
    w3b,
    slope_buf,
    back_buf,
    acc_one,
    acc_two,
    acc_three,
    rows_f32,
    e_send,
    e_recv,
    p2_send,
    p2_recv,
    p3_send,
    p3_recv,
    z2,
    z3,
    a2,
    a3,
    s1,
    y1,
    stats,
    plane_ssem,
    plane_rsem,
    z_ssem,
    z_rsem,
):
    g = lax.axis_index("grp")
    s = lax.axis_index("shard")
    width = emb_grads.shape[1]
    block_rows = 8
    count = touched.shape[1]
    slots = block_slot.shape[1]
    local_blocks = slot_table.shape[1]
    tokens = x.shape[1]
    din = x.shape[0]

    barrier = pltpu.get_barrier_semaphore()
    for k in range(1, shards):
        pl.semaphore_signal(barrier, inc=1, device_id=(g, lax.rem(s + k, shards)), device_id_type=MESH)
    for k in range(1, grps):
        pl.semaphore_signal(barrier, inc=1, device_id=(lax.rem(g + k, grps), s), device_id_type=MESH)

    def plane(phase, k, src, dst):
        return pltpu.make_async_remote_copy(
            src_ref=src,
            dst_ref=dst,
            send_sem=plane_ssem.at[phase, k],
            recv_sem=plane_rsem.at[phase, k],
            device_id=(g, lax.rem(s + k, shards)),
            device_id_type=MESH,
        )

    def along(phase, k, src, dst):
        return pltpu.make_async_remote_copy(
            src_ref=src,
            dst_ref=dst,
            send_sem=z_ssem.at[phase, k],
            recv_sem=z_rsem.at[phase, k],
            device_id=(lax.rem(g + k, grps), s),
            device_id_type=MESH,
        )

    def plane_scatter(phase, src, dst):
        out = [plane(phase, k, src.at[lax.rem(s + k, shards)], dst.at[s]) for k in range(1, shards)]
        for c in out:
            c.start()
        return out

    def plane_spread(phase, buf):
        out = [plane(phase, k, buf.at[s], buf.at[s]) for k in range(1, shards)]
        for c in out:
            c.start()
        return out

    def z_spread(phase, buf):
        out = [along(phase, k, buf.at[g], buf.at[g]) for k in range(1, grps)]
        for c in out:
            c.start()
        return out

    def recv(copies):
        for c in copies:
            c.wait_recv()

    eye = square_eye(count)
    touched_col = to_col(touched[...].astype(F32), eye)
    hot = touched_col == iota((count, slots), 1)
    slot_col = jnp.sum(jnp.where(hot, block_slot[...].astype(F32), 0.0), axis=1, keepdims=True)
    slot_row = to_row(slot_col, eye)
    owner_col = jnp.floor((slot_col + 0.5) / local_blocks)
    owner_row = jnp.floor((slot_row + 0.5) / local_blocks)
    local_row = slot_row - owner_row * local_blocks
    earlier = (owner_col == owner_row) & (iota((count, count), 0) < iota((count, count), 1))
    rank_row = jnp.sum(jnp.where(earlier, 1.0, 0.0), axis=0, keepdims=True)
    send_row = owner_row * CAP + rank_row
    picker = iota((shards * CAP, count), 0) == send_row
    pick_f32 = jnp.where(picker, 1.0, 0.0)
    pick_bf = pick_f32.astype(BF16)
    filled = jnp.sum(pick_f32, axis=1, keepdims=True)
    local_col = jnp.sum(jnp.where(picker, local_row, 0.0), axis=1, keepdims=True)
    local_col = jnp.where(filled > 0.5, local_col, -1.0)
    rows_f32[...] = emb_grads[...].astype(F32)
    for r in range(block_rows):
        part = rows_f32[pl.ds(r, count, stride=block_rows), :].astype(BF16)
        picked = mm(pick_bf, part).reshape(shards, CAP, width)
        e_send[:, :, r * width : (r + 1) * width] = picked.astype(BF16)
    lanes = jnp.broadcast_to(local_col, (shards * CAP, width)).reshape(shards, CAP, width)
    e_send[:, :, block_rows * width :] = lanes.astype(BF16)
    e_recv[g, s] = e_send[s]

    pl.semaphore_wait(barrier, shards + grps - 2)
    sends = []
    e_plane = [
        plane(0, k, e_send.at[lax.rem(s + k, shards)], e_recv.at[g, s]) for k in range(1, shards)
    ]
    for c in e_plane:
        c.start()
    sends += e_plane

    w1t[...] = w_one[...].T.astype(BF16)
    w2t[...] = w_two[...].T.astype(BF16)
    w2b[...] = w_two[...].astype(BF16)
    w3b[...] = w_three[...].astype(BF16)
    acc_one[...] = jnp.zeros_like(acc_one)
    acc_two[...] = jnp.zeros_like(acc_two)
    acc_three[...] = jnp.zeros_like(acc_three)

    def forward(i, carry):
        tok = pl.ds(pl.multiple_of(i * chunk, chunk), chunk)
        hid, slope = gate(mm(w1t[...], x[:, tok]))
        hidden_one = hid.astype(BF16)
        slope_buf[:, tok] = slope
        hid, slope = gate(mm(w2t[...], hidden_one))
        c = cot[tok, :]
        acc_three[...] += mm(hid.astype(BF16), c)
        back = (mm(w3b[...], c, NT) * slope).astype(BF16)
        back_buf[:, tok] = back
        acc_two[...] += mm(hidden_one, back, NT)
        return carry

    def backward(i, carry):
        tok = pl.ds(pl.multiple_of(i * chunk, chunk), chunk)
        back = (mm(w2b[...], back_buf[:, tok]) * slope_buf[:, tok]).astype(BF16)
        acc_one[0:din, :] += mm(x[:, tok], back, NT)
        return carry

    steps = tokens // chunk
    head = steps // 2
    lax.fori_loop(0, head, forward, 0)
    recv(e_plane)
    e_z = z_spread(0, e_recv)
    sends += e_z
    lax.fori_loop(head, steps, forward, 0)

    p2_send[...] = acc_two[...].reshape(p2_send.shape).astype(BF16)
    p3_send[...] = acc_three[...].reshape(p3_send.shape).astype(BF16)
    p2_recv[s] = p2_send[s]
    p3_recv[s] = p3_send[s]
    c_p2 = plane_scatter(1, p2_send, p2_recv)
    c_p3 = plane_scatter(2, p3_send, p3_recv)
    sends += c_p2 + c_p3

    lax.fori_loop(0, steps, backward, 0)
    s1[s] = acc_one[...].astype(BF16)
    c_s1 = plane_spread(3, s1)
    sends += c_s1

    def total(buf, n):
        out = buf[0].astype(F32)
        for i in range(1, n):
            out += buf[i].astype(F32)
        return out

    recv(c_p2)
    z2[g] = total(p2_recv, shards).astype(BF16)
    c_z2 = z_spread(1, z2)
    recv(c_p3)
    z3[g] = total(p3_recv, shards).astype(BF16)
    c_z3 = z_spread(2, z3)
    recv(c_s1)
    y1[g] = total(s1, shards).astype(BF16)
    c_y1 = z_spread(3, y1)
    sends += c_z2 + c_z3 + c_y1

    recv(e_z)
    pieces = grps * shards * CAP
    row_width = block_rows * width
    tags = e_recv[:, :, :, row_width:].astype(F32).reshape(pieces, width)
    match = jnp.where(tags[:, 0:1] == iota((pieces, local_blocks), 1), 1.0, 0.0)
    match_t = match.T.astype(BF16)
    hits = mm(match_t, jnp.ones((pieces, width), BF16)) > 0.5
    row_weight = jnp.zeros((local_blocks, width), F32)
    row_update = jnp.zeros((local_blocks, width), F32)
    for r in range(block_rows):
        at = pl.ds(r, local_blocks, stride=block_rows)
        rows = e_recv[:, :, :, r * width : (r + 1) * width].astype(F32)
        summed = mm(match_t, rows.reshape(pieces, width).astype(BF16))
        emb_out[at, :] = summed
        weight = table[at, :]
        update = adam(table_first[at, :], table_second[at, :], summed, weight)[2]
        update = jnp.where(hits, update, 0.0)
        row_weight += weight * weight
        row_update += update * update
    slot_eye = square_eye(local_blocks)
    table_col = to_col(slot_table[...].astype(F32), slot_eye)
    table_hot = table_col == iota((local_blocks, 128), 1)
    weight_col = jnp.sum(row_weight, axis=1, keepdims=True)
    update_col = jnp.sum(row_update, axis=1, keepdims=True)
    stats[s] = jnp.concatenate(
        [
            jnp.sum(jnp.where(table_hot, weight_col, 0.0), axis=0, keepdims=True),
            jnp.sum(jnp.where(table_hot, update_col, 0.0), axis=0, keepdims=True),
            jnp.zeros((6, 128), F32),
        ],
        axis=0,
    )
    c_st = plane_spread(4, stats)
    sends += c_st

    recv(c_z2)
    a2[s] = total(z2, grps).astype(BF16)
    c_a2 = plane_spread(5, a2)
    recv(c_z3)
    a3[s] = total(z3, grps).astype(BF16)
    c_a3 = plane_spread(6, a3)
    sends += c_a2 + c_a3
    recv(c_st)
    tot = total(stats, shards)
    ratio = jnp.sqrt(tot[0:1]) / (jnp.sqrt(tot[1:2]) + ratio_eps)
    ratio_col = jnp.sum(jnp.where(table_hot, ratio, 0.0), axis=1, keepdims=True)
    rate = jnp.where(hits, learn_rate * ratio_col, -1.0)
    for r in range(block_rows):
        rate_out[pl.ds(r, local_blocks, stride=block_rows), :] = rate
    recv(c_y1)
    g_one[...] = total(y1, grps)
    recv(c_a2)
    g_two[...] = a2[...].astype(F32).reshape(g_two.shape)
    recv(c_a3)
    g_three[...] = a3[...].astype(F32).reshape(g_three.shape)
    for c in sends:
        c.wait_send()


def lamb_kernel(
    emb, rate, table, tf, ts, g1, g2, g3, w1, w2, w3, f1, f2, f3, q1, q2, q3,
    o_t, o_tf, o_ts, o_w1, o_w2, o_w3, o_f1, o_f2, o_f3, o_q1, o_q2, o_q3,
):
    mask = rate[...] >= 0.0
    first, second, update = adam(tf[...], ts[...], emb[...], table[...])
    o_tf[...] = jnp.where(mask, first, tf[...])
    o_ts[...] = jnp.where(mask, second, ts[...])
    o_t[...] = jnp.where(mask, table[...] - rate[...] * update, table[...])
    for grad, w, f, q, ow, of, oq in (
        (g1, w1, f1, q1, o_w1, o_f1, o_q1),
        (g2, w2, f2, q2, o_w2, o_f2, o_q2),
        (g3, w3, f3, q3, o_w3, o_f3, o_q3),
    ):
        weight = w[...]
        first, second, update = adam(f[...], q[...], grad[0 : w.shape[0], :], weight)
        of[...] = first
        oq[...] = second
        trust = jnp.sqrt(jnp.sum(weight * weight, keepdims=True)) / (
            jnp.sqrt(jnp.sum(update * update, keepdims=True)) + ratio_eps
        )
        ow[...] = weight - learn_rate * trust * update


def body(
    table, table_first, table_second, slot_table, touched, emb_grads, block_slot,
    dense_x, dense_cot, w_one, w_two, w_three, first_one, first_two, first_three,
    second_one, second_two, second_three,
):
    shards = lax.axis_size("shard")
    grps = lax.axis_size("grp")
    blocks, block_rows, width = table.shape
    count = touched.shape[1]
    din, tokens = dense_x.shape
    h_one, h_two = w_two.shape
    out_dim = w_three.shape[1]
    chunk = min(512, tokens)
    din_pad = -(-din // 16) * 16
    flat = (blocks * block_rows, width)
    e_width = block_rows * width + width
    r2 = h_one // shards
    r3 = h_two // shards
    vmem = pl.BlockSpec(memory_space=pltpu.VMEM)
    t2, tf2, ts2 = (a.reshape(flat) for a in (table, table_first, table_second))
    sds = jax.ShapeDtypeStruct
    emb, rate, g1, g2, g3 = pl.pallas_call(
        functools.partial(exchange_kernel, grps, shards, chunk),
        out_shape=(
            sds(flat, F32),
            sds(flat, F32),
            sds((din_pad, h_one), F32),
            sds((h_one, h_two), F32),
            sds((h_two, out_dim), F32),
        ),
        in_specs=[vmem] * 12,
        out_specs=(vmem,) * 5,
        scratch_shapes=[
            pltpu.VMEM((h_one, din), BF16),
            pltpu.VMEM((h_two, h_one), BF16),
            pltpu.VMEM((h_one, h_two), BF16),
            pltpu.VMEM((h_two, out_dim), BF16),
            pltpu.VMEM((h_one, tokens), F32),
            pltpu.VMEM((h_two, tokens), BF16),
            pltpu.VMEM((din_pad, h_one), F32),
            pltpu.VMEM((h_one, h_two), F32),
            pltpu.VMEM((h_two, out_dim), F32),
            pltpu.VMEM((count * block_rows, width), F32),
            pltpu.VMEM((shards, CAP, e_width), BF16),
            pltpu.VMEM((grps, shards, CAP, e_width), BF16),
            pltpu.VMEM((shards, r2, h_two), BF16),
            pltpu.VMEM((shards, r2, h_two), BF16),
            pltpu.VMEM((shards, r3, out_dim), BF16),
            pltpu.VMEM((shards, r3, out_dim), BF16),
            pltpu.VMEM((grps, r2, h_two), BF16),
            pltpu.VMEM((grps, r3, out_dim), BF16),
            pltpu.VMEM((shards, r2, h_two), BF16),
            pltpu.VMEM((shards, r3, out_dim), BF16),
            pltpu.VMEM((shards, din_pad, h_one), BF16),
            pltpu.VMEM((grps, din_pad, h_one), BF16),
            pltpu.VMEM((shards, 8, 128), F32),
            pltpu.SemaphoreType.DMA((7, shards)),
            pltpu.SemaphoreType.DMA((7, shards)),
            pltpu.SemaphoreType.DMA((4, grps)),
            pltpu.SemaphoreType.DMA((4, grps)),
        ],
        compiler_params=pltpu.CompilerParams(collective_id=0, has_side_effects=True),
        name="tower_exchange",
    )(
        touched,
        block_slot.reshape(1, -1),
        slot_table.reshape(1, -1),
        emb_grads.reshape(count * block_rows, width),
        dense_x,
        dense_cot,
        w_one,
        w_two,
        w_three,
        t2,
        tf2,
        ts2,
    )
    mats = (w_one, w_two, w_three)
    outs = pl.pallas_call(
        lamb_kernel,
        out_shape=(sds(flat, F32),) * 3 + tuple(sds(w.shape, F32) for w in mats * 3),
        in_specs=[vmem] * 17,
        out_specs=(vmem,) * 12,
        name="lamb",
    )(
        emb, rate, t2, tf2, ts2, g1, g2, g3, w_one, w_two, w_three,
        first_one, first_two, first_three, second_one, second_two, second_three,
    )
    return tuple(o.reshape(table.shape) for o in outs[:3]) + tuple(outs[3:])


def solution(mesh):
    dense = (P(),) * 9
    rows = P("shard", None, None)
    return jax.shard_map(
        body,
        mesh=mesh,
        in_specs=(
            rows,
            rows,
            rows,
            P("shard"),
            P("grp", "shard"),
            P("grp", "shard", None, None),
            P(),
            P(None, ("grp", "shard")),
            P(("grp", "shard"), None),
        )
        + dense,
        out_specs=(rows,) * 3 + dense,
        check_vma=False,
    )
```

time: 180 us -> 44.3 us (0.25)
  blocking collectives: 82 us -> 0 us
  Pallas kernels: 0 us -> 43.5 us
  matrix products: 25.8 us -> 0 us
  waiting for transfers between devices: 21.3 us -> 0 us
  between operations: 18.6 us -> 0.66 us
  other arithmetic: 12.7 us -> 0 us
  local copies, waits for them, and re-layouts: 10.6 us -> 0 us
  starting transfers between devices: 8.81 us -> 0 us
    psum x2 -> x0, blocking collectives: 52.8 us -> none  [the longest x1 41 us: body(): lax.psum((dense_terms[0], dense_terms[1], dense_terms[2]), ('grp', 'shard'))]
    pallas_call x0 -> x2, Pallas kernels: none -> 43.5 us  [the longest x1 37.7 us: body(): pl.pallas_call(functools.partial(exchange_kernel, grps, shards, chunk), o...]
    all_gather x2 -> x0, blocking collectives: 29.2 us -> none  [the longest x1 16 us: body(): lax.all_gather(recv_rows, 'grp', axis=0, tiled=True).reshape(-1, row_width)]
    dot_general x11 -> x0, matrix products: 25.8 us -> none  [the longest x1 7.68 us: tower_grads(): grad_one = jnp.dot(dense_x, back_one, preferred_element_type=jnp.float32)]
    psum x1 -> x0, waiting for transfers between devices: 21.3 us -> none  [body(): lax.psum((dense_terms[0], dense_terms[1], dense_terms[2]), ('grp', 'shard'))]
    all_to_all x2 -> x0, starting transfers between devices: 8.77 us -> none  [the longest x1 5.2 us: body(): lax.all_to_all(send_local, 'shard', split_axis=0, concat_axis=0, tiled=True)]
    unnamed x46 -> x0, local copies, waits for them, and re-layouts: 6.98 us -> none
    reduce_sum x7 -> x0, other arithmetic: 6.09 us -> none  [the longest x3 4.67 us: lamb_dense(): jnp.sum(update * update)]
  transfers between devices with their start and end apart: 3 -> 0, of which waited for: 1 -> 0; matrix products, arithmetic and copies ran while one was open for 21% -> 0% of each run, Pallas kernels for 0% -> 0%
where the time goes in v1:
time: 44.3 us; the launch traced here: 44.2 us
  Pallas kernels  43.5 us (98%)
  between operations  0.66 us (1%)
    pallas_call x1, Pallas kernels, body(): pl.pallas_call(functools.partial(exchange_kernel, grps, shards, chunk), o...  37.7 us
    pallas_call x1, Pallas kernels, body(): pl.pallas_call(lamb_kernel, out_shape=(sds(flat, F32),) * 3 + tuple((sds(...  5.87 us

profile of v1, /device:TPU:0, one launch (start us, length us, event | category | flops | bytes accessed | tf_op | source)
XLA Modules:
  0.0 44.2 jit_solution(5411114641621872777)
XLA Ops:
  0.6 37.7 %tower_exchange.1 = (f32[1024,128]{1,0:T(8,128)}, f32[1024,128]{1,0:T(8,128)}, f32[16,512]{1,0:T(8,128)}, f32[512,256]{1,0:T(8,128)}, f32[256,128]{1,0:T(8,128)}) custom-call(s32[1,32]{1,0:T(1,128)} %touched.1, s32[1,1024]{1,0:T(1,128)} %bitcast.16, s32[1,128]{1,0:T(1,128)} %bitcast.17, bf16[256,128]{1,0:T(8,128)(2,1)} %bitcast.15, bf16[13,4096]{1,0:T(8,128)(2,1)} %x.1, ...), custom_call_target="tpu_custom_call" | custom-call | tf_op jit(solution)/shard_map/tower_exchange/pallas_call | solution.py:376
  38.3 5.9 %lamb.1 = (f32[1024,128]{1,0:T(8,128)}, f32[1024,128]{1,0:T(8,128)}, f32[1024,128]{1,0:T(8,128)}, f32[13,512]{1,0:T(8,128)}, f32[512,256]{1,0:T(8,128)}, /*index...) custom-call(f32[1024,128]{1,0:T(8,128)} %get-tuple-element.29.emb, ...), custom_call_target="tpu_custom_call" | custom-call | tf_op jit(solution)/shard_map/lamb/pallas_call | solution.py:433

commit v2 on v1

--- a/solution.py
+++ b/solution.py
@@ -8,6 +8,7 @@
 
 TABLES = 26
 CAP = 8
+HEAD = 1
 
 beta_one = 0.9
 beta_two = 0.999
@@ -70,14 +71,14 @@
     block_slot,
     slot_table,
     emb_grads,
-    x,
-    cot,
     w_one,
-    w_two,
     w_three,
-    table,
-    table_first,
-    table_second,
+    w_two_in,
+    x_in,
+    cot_in,
+    table_in,
+    first_in,
+    second_in,
     emb_out,
     rate_out,
     g_one,
@@ -93,8 +94,17 @@
     acc_two,
     acc_three,
     rows_f32,
+    w_two,
+    x,
+    cot,
+    table,
+    table_first,
+    table_second,
     e_send,
     e_recv,
+    t_send,
+    t_recv,
+    t_all,
     p2_send,
     p2_recv,
     p3_send,
@@ -110,6 +120,7 @@
     plane_rsem,
     z_ssem,
     z_rsem,
+    load_sem,
 ):
     g = lax.axis_index("grp")
     s = lax.axis_index("shard")
@@ -121,6 +132,21 @@
     tokens = x.shape[1]
     din = x.shape[0]
 
+    loads = [
+        pltpu.make_async_copy(src, dst, load_sem.at[i])
+        for i, (src, dst) in enumerate(
+            (
+                (w_two_in, w_two),
+                (x_in, x),
+                (cot_in, cot),
+                (table_in, table),
+                (first_in, table_first),
+                (second_in, table_second),
+            )
+        )
+    ]
+    for c in loads:
+        c.start()
     barrier = pltpu.get_barrier_semaphore()
     for k in range(1, shards):
         pl.semaphore_signal(barrier, inc=1, device_id=(g, lax.rem(s + k, shards)), device_id_type=MESH)
@@ -192,8 +218,9 @@
         picked = mm(pick_bf, part).reshape(shards, CAP, width)
         e_send[:, :, r * width : (r + 1) * width] = picked.astype(BF16)
     lanes = jnp.broadcast_to(local_col, (shards * CAP, width)).reshape(shards, CAP, width)
-    e_send[:, :, block_rows * width :] = lanes.astype(BF16)
+    t_send[...] = lanes.astype(BF16)
     e_recv[g, s] = e_send[s]
+    t_recv[s] = t_send[s]
 
     pl.semaphore_wait(barrier, shards + grps - 2)
     sends = []
@@ -202,8 +229,11 @@
     ]
     for c in e_plane:
         c.start()
-    sends += e_plane
-
+    t_plane = plane_scatter(1, t_send, t_recv)
+    sends += e_plane + t_plane
+
+    for c in loads[:3]:
+        c.wait()
     w1t[...] = w_one[...].T.astype(BF16)
     w2t[...] = w_two[...].T.astype(BF16)
     w2b[...] = w_two[...].astype(BF16)
@@ -232,56 +262,84 @@
         return carry
 
     steps = tokens // chunk
-    head = steps // 2
+    head = min(HEAD, steps)
     lax.fori_loop(0, head, forward, 0)
     recv(e_plane)
     e_z = z_spread(0, e_recv)
-    sends += e_z
+    recv(t_plane)
+    group = shards * CAP
+    tag_lanes = t_all.shape[2]
+    tag_eye = iota((group, tag_lanes), 0) == iota((group, tag_lanes), 1)
+    tag_row = to_row(t_recv[...].astype(F32).reshape(group, width)[:, 0:1], tag_eye)
+    t_all[g] = jnp.broadcast_to(tag_row, t_all.shape[1:]).astype(BF16)
+    t_z = z_spread(1, t_all)
+    sends += e_z + t_z
     lax.fori_loop(head, steps, forward, 0)
 
+    p3_send[...] = acc_three[...].reshape(p3_send.shape).astype(BF16)
+    p3_recv[s] = p3_send[s]
+    c_p3 = plane_scatter(2, p3_send, p3_recv)
     p2_send[...] = acc_two[...].reshape(p2_send.shape).astype(BF16)
-    p3_send[...] = acc_three[...].reshape(p3_send.shape).astype(BF16)
     p2_recv[s] = p2_send[s]
-    p3_recv[s] = p3_send[s]
-    c_p2 = plane_scatter(1, p2_send, p2_recv)
-    c_p3 = plane_scatter(2, p3_send, p3_recv)
-    sends += c_p2 + c_p3
+    parts = p2_send.shape[1]
+    c_p2 = []
+    for h in range(parts):
+        group_p = [
+            plane(6 + h, k, p2_send.at[lax.rem(s + k, shards), h], p2_recv.at[s, h])
+            for k in range(1, shards)
+        ]
+        for c in group_p:
+            c.start()
+        c_p2.append(group_p)
+        sends += group_p
+    sends += c_p3
 
     lax.fori_loop(0, steps, backward, 0)
     s1[s] = acc_one[...].astype(BF16)
     c_s1 = plane_spread(3, s1)
     sends += c_s1
 
-    def total(buf, n):
-        out = buf[0].astype(F32)
+    def total(buf, n, *at):
+        out = buf[(0,) + at].astype(F32)
         for i in range(1, n):
-            out += buf[i].astype(F32)
+            out += buf[(i,) + at].astype(F32)
         return out
 
-    recv(c_p2)
-    z2[g] = total(p2_recv, shards).astype(BF16)
-    c_z2 = z_spread(1, z2)
+    def start(copies):
+        for c in copies:
+            c.start()
+        sends.extend(copies)
+        return copies
+
     recv(c_p3)
     z3[g] = total(p3_recv, shards).astype(BF16)
     c_z3 = z_spread(2, z3)
+    c_z2 = []
+    for h in range(parts):
+        recv(c_p2[h])
+        z2[g, h] = total(p2_recv, shards, h).astype(BF16)
+        c_z2.append(start([along(4 + h, k, z2.at[g, h], z2.at[g, h]) for k in range(1, grps)]))
     recv(c_s1)
     y1[g] = total(s1, shards).astype(BF16)
     c_y1 = z_spread(3, y1)
-    sends += c_z2 + c_z3 + c_y1
-
+    sends += c_z3 + c_y1
+
+    slots_at = iota((local_blocks, group), 0)
     recv(e_z)
-    pieces = grps * shards * CAP
-    row_width = block_rows * width
-    tags = e_recv[:, :, :, row_width:].astype(F32).reshape(pieces, width)
-    match = jnp.where(tags[:, 0:1] == iota((pieces, local_blocks), 1), 1.0, 0.0)
-    match_t = match.T.astype(BF16)
-    hits = mm(match_t, jnp.ones((pieces, width), BF16)) > 0.5
+    recv(t_z)
+    for c in loads[3:]:
+        c.wait()
+    matches = [
+        jnp.where(slots_at == t_all[q, 0:1, 0:group].astype(F32), 1.0, 0.0) for q in range(grps)
+    ]
+    hits = jnp.sum(sum(matches), axis=1, keepdims=True) > 0.5
+    match_t = jnp.concatenate(matches, axis=1).astype(BF16)
     row_weight = jnp.zeros((local_blocks, width), F32)
     row_update = jnp.zeros((local_blocks, width), F32)
     for r in range(block_rows):
         at = pl.ds(r, local_blocks, stride=block_rows)
         rows = e_recv[:, :, :, r * width : (r + 1) * width].astype(F32)
-        summed = mm(match_t, rows.reshape(pieces, width).astype(BF16))
+        summed = mm(match_t, rows.reshape(grps * group, width).astype(BF16))
         emb_out[at, :] = summed
         weight = table[at, :]
         update = adam(table_first[at, :], table_second[at, :], summed, weight)[2]
@@ -304,18 +362,23 @@
     c_st = plane_spread(4, stats)
     sends += c_st
 
-    recv(c_z2)
-    a2[s] = total(z2, grps).astype(BF16)
-    c_a2 = plane_spread(5, a2)
     recv(c_z3)
     a3[s] = total(z3, grps).astype(BF16)
-    c_a3 = plane_spread(6, a3)
-    sends += c_a2 + c_a3
+    c_a3 = plane_spread(5, a3)
+    sends += c_a3
+    c_a2 = []
+    for h in range(parts):
+        recv(c_z2[h])
+        a2[s, h] = total(z2, grps, h).astype(BF16)
+        c_a2 += start(
+            [plane(6 + parts + h, k, a2.at[s, h], a2.at[s, h]) for k in range(1, shards)]
+        )
     recv(c_st)
     tot = total(stats, shards)
     ratio = jnp.sqrt(tot[0:1]) / (jnp.sqrt(tot[1:2]) + ratio_eps)
     ratio_col = jnp.sum(jnp.where(table_hot, ratio, 0.0), axis=1, keepdims=True)
     rate = jnp.where(hits, learn_rate * ratio_col, -1.0)
+    rate = jnp.broadcast_to(rate, (local_blocks, width))
     for r in range(block_rows):
         rate_out[pl.ds(r, local_blocks, stride=block_rows), :] = rate
     recv(c_y1)
@@ -328,28 +391,46 @@
         c.wait_send()
 
 
-def lamb_kernel(
-    emb, rate, table, tf, ts, g1, g2, g3, w1, w2, w3, f1, f2, f3, q1, q2, q3,
-    o_t, o_tf, o_ts, o_w1, o_w2, o_w3, o_f1, o_f2, o_f3, o_q1, o_q2, o_q3,
-):
-    mask = rate[...] >= 0.0
-    first, second, update = adam(tf[...], ts[...], emb[...], table[...])
-    o_tf[...] = jnp.where(mask, first, tf[...])
-    o_ts[...] = jnp.where(mask, second, ts[...])
-    o_t[...] = jnp.where(mask, table[...] - rate[...] * update, table[...])
-    for grad, w, f, q, ow, of, oq in (
-        (g1, w1, f1, q1, o_w1, o_f1, o_q1),
-        (g2, w2, f2, q2, o_w2, o_f2, o_q2),
-        (g3, w3, f3, q3, o_w3, o_f3, o_q3),
-    ):
+def lamb_kernel(*refs):
+    ins, outs = refs[:17], refs[17:29]
+    bufs, stage = refs[29:46], refs[46:58]
+    in_sem, out_sem = refs[58:]
+    loads = [pltpu.make_async_copy(a, b, in_sem.at[i]) for i, (a, b) in enumerate(zip(ins, bufs))]
+    stores = [
+        pltpu.make_async_copy(a, b, out_sem.at[i]) for i, (a, b) in enumerate(zip(stage, outs))
+    ]
+    dense = [(5 + j, 8 + j, 11 + j, 14 + j) for j in (1, 0, 2)]
+    for group in dense + [range(5)]:
+        for i in group:
+            loads[i].start()
+    for j, group in zip((1, 0, 2), dense):
+        for i in group:
+            loads[i].wait()
+        grad, w, f, q = (bufs[i] for i in group)
         weight = w[...]
-        first, second, update = adam(f[...], q[...], grad[0 : w.shape[0], :], weight)
-        of[...] = first
-        oq[...] = second
+        first, second, update = adam(f[...], q[...], grad[0 : w.shape[0], :].astype(F32), weight)
+        stage[6 + j][...] = first
+        stage[9 + j][...] = second
+        stores[6 + j].start()
+        stores[9 + j].start()
         trust = jnp.sqrt(jnp.sum(weight * weight, keepdims=True)) / (
             jnp.sqrt(jnp.sum(update * update, keepdims=True)) + ratio_eps
         )
-        ow[...] = weight - learn_rate * trust * update
+        stage[3 + j][...] = weight - learn_rate * trust * update
+        stores[3 + j].start()
+    for i in range(5):
+        loads[i].wait()
+    emb, rate, table, tf, ts = bufs[:5]
+    mask = rate[...] >= 0.0
+    first, second, update = adam(tf[...], ts[...], emb[...], table[...])
+    stage[1][...] = jnp.where(mask, first, tf[...])
+    stores[1].start()
+    stage[2][...] = jnp.where(mask, second, ts[...])
+    stores[2].start()
+    stage[0][...] = jnp.where(mask, table[...] - rate[...] * update, table[...])
+    stores[0].start()
+    for c in stores:
+        c.wait()
 
 
 def body(
@@ -364,12 +445,15 @@
     din, tokens = dense_x.shape
     h_one, h_two = w_two.shape
     out_dim = w_three.shape[1]
-    chunk = min(512, tokens)
+    chunk = min(1024, tokens)
     din_pad = -(-din // 16) * 16
     flat = (blocks * block_rows, width)
-    e_width = block_rows * width + width
+    e_width = block_rows * width
+    tag_width = max(128, shards * CAP)
     r2 = h_one // shards
     r3 = h_two // shards
+    parts = min(4, max(1, r2 // 16))
+    anywhere = pl.BlockSpec(memory_space=pl.ANY)
     vmem = pl.BlockSpec(memory_space=pltpu.VMEM)
     t2, tf2, ts2 = (a.reshape(flat) for a in (table, table_first, table_second))
     sds = jax.ShapeDtypeStruct
@@ -382,7 +466,7 @@
             sds((h_one, h_two), F32),
             sds((h_two, out_dim), F32),
         ),
-        in_specs=[vmem] * 12,
+        in_specs=[vmem] * 6 + [anywhere] * 6,
         out_specs=(vmem,) * 5,
         scratch_shapes=[
             pltpu.VMEM((h_one, din), BF16),
@@ -395,23 +479,33 @@
             pltpu.VMEM((h_one, h_two), F32),
             pltpu.VMEM((h_two, out_dim), F32),
             pltpu.VMEM((count * block_rows, width), F32),
+            pltpu.VMEM(w_two.shape, F32),
+            pltpu.VMEM(dense_x.shape, BF16),
+            pltpu.VMEM(dense_cot.shape, BF16),
+            pltpu.VMEM(flat, F32),
+            pltpu.VMEM(flat, F32),
+            pltpu.VMEM(flat, F32),
             pltpu.VMEM((shards, CAP, e_width), BF16),
             pltpu.VMEM((grps, shards, CAP, e_width), BF16),
-            pltpu.VMEM((shards, r2, h_two), BF16),
-            pltpu.VMEM((shards, r2, h_two), BF16),
+            pltpu.VMEM((shards, CAP, width), BF16),
+            pltpu.VMEM((shards, CAP, width), BF16),
+            pltpu.VMEM((grps, 16, tag_width), BF16),
+            pltpu.VMEM((shards, parts, r2 // parts, h_two), BF16),
+            pltpu.VMEM((shards, parts, r2 // parts, h_two), BF16),
             pltpu.VMEM((shards, r3, out_dim), BF16),
             pltpu.VMEM((shards, r3, out_dim), BF16),
-            pltpu.VMEM((grps, r2, h_two), BF16),
+            pltpu.VMEM((grps, parts, r2 // parts, h_two), BF16),
             pltpu.VMEM((grps, r3, out_dim), BF16),
-            pltpu.VMEM((shards, r2, h_two), BF16),
+            pltpu.VMEM((shards, parts, r2 // parts, h_two), BF16),
             pltpu.VMEM((shards, r3, out_dim), BF16),
             pltpu.VMEM((shards, din_pad, h_one), BF16),
             pltpu.VMEM((grps, din_pad, h_one), BF16),
             pltpu.VMEM((shards, 8, 128), F32),
-            pltpu.SemaphoreType.DMA((7, shards)),
-            pltpu.SemaphoreType.DMA((7, shards)),
-            pltpu.SemaphoreType.DMA((4, grps)),
-            pltpu.SemaphoreType.DMA((4, grps)),
+            pltpu.SemaphoreType.DMA((6 + 2 * parts, shards)),
+            pltpu.SemaphoreType.DMA((6 + 2 * parts, shards)),
+            pltpu.SemaphoreType.DMA((4 + parts, grps)),
+            pltpu.SemaphoreType.DMA((4 + parts, grps)),
+            pltpu.SemaphoreType.DMA((6,)),
         ],
         compiler_params=pltpu.CompilerParams(collective_id=0, has_side_effects=True),
         name="tower_exchange",
@@ -420,26 +514,30 @@
         block_slot.reshape(1, -1),
         slot_table.reshape(1, -1),
         emb_grads.reshape(count * block_rows, width),
+        w_one,
+        w_three,
+        w_two,
         dense_x,
         dense_cot,
-        w_one,
-        w_two,
-        w_three,
         t2,
         tf2,
         ts2,
     )
     mats = (w_one, w_two, w_three)
-    outs = pl.pallas_call(
-        lamb_kernel,
-        out_shape=(sds(flat, F32),) * 3 + tuple(sds(w.shape, F32) for w in mats * 3),
-        in_specs=[vmem] * 17,
-        out_specs=(vmem,) * 12,
-        name="lamb",
-    )(
+    args = (
         emb, rate, t2, tf2, ts2, g1, g2, g3, w_one, w_two, w_three,
         first_one, first_two, first_three, second_one, second_two, second_three,
     )
+    shapes = (sds(flat, F32),) * 3 + tuple(sds(w.shape, F32) for w in mats * 3)
+    outs = pl.pallas_call(
+        lamb_kernel,
+        out_shape=shapes,
+        in_specs=[anywhere] * 17,
+        out_specs=(anywhere,) * 12,
+        scratch_shapes=[pltpu.VMEM(a.shape, a.dtype) for a in args + shapes]
+        + [pltpu.SemaphoreType.DMA((17,)), pltpu.SemaphoreType.DMA((12,))],
+        name="lamb",
+    )(*args)
     return tuple(o.reshape(table.shape) for o in outs[:3]) + tuple(outs[3:])
 
 

time: 44.3 us -> 42.3 us (0.955)
  Pallas kernels: 43.5 us -> 41.5 us
    pallas_call x1, Pallas kernels: 5.87 us -> 4.82 us  [body(): pl.pallas_call(lamb_kernel, out_shape=shapes, in_specs=[anywhere] * 17, o...]
    pallas_call x1, Pallas kernels: 37.7 us -> 36.6 us  [body(): pl.pallas_call(functools.partial(exchange_kernel, grps, shards, chunk), o...]
where the time goes in v2:
time: 42.3 us; the launch traced here: 42.1 us
  Pallas kernels  41.5 us (98%)
  between operations  0.66 us (2%)
    pallas_call x1, Pallas kernels, body(): pl.pallas_call(functools.partial(exchange_kernel, grps, shards, chunk), o...  36.6 us
    pallas_call x1, Pallas kernels, body(): pl.pallas_call(lamb_kernel, out_shape=shapes, in_specs=[anywhere] * 17, o...  4.82 us

profile of v2, /device:TPU:0, one launch (start us, length us, event | category | flops | bytes accessed | tf_op | source)
XLA Modules:
  0.0 42.1 jit_solution(8101868361852420799)
XLA Ops:
  0.6 36.6 %tower_exchange.1 = (f32[1024,128]{1,0:T(8,128)}, f32[1024,128]{1,0:T(8,128)}, f32[16,512]{1,0:T(8,128)}, f32[512,256]{1,0:T(8,128)}, f32[256,128]{1,0:T(8,128)}) custom-call(s32[1,32]{1,0:T(1,128)} %touched.1, s32[1,1024]{1,0:T(1,128)} %bitcast.16, s32[1,128]{1,0:T(1,128)} %bitcast.17, bf16[256,128]{1,0:T(8,128)(2,1)} %bitcast.15, f32[13,512]{1,0:T(8,128)} %refs_8_.1, ...), custom_call_target="tpu_custom_call" | custom-call | tf_op jit(solution)/shard_map/tower_exchange/pallas_call | solution.py:460
  37.3 4.8 %lamb.1 = (f32[1024,128]{1,0:T(8,128)}, f32[1024,128]{1,0:T(8,128)}, f32[1024,128]{1,0:T(8,128)}, f32[13,512]{1,0:T(8,128)}, f32[512,256]{1,0:T(8,128)}, /*index...) custom-call(f32[1024,128]{1,0:T(8,128)} %get-tuple-element.29.refs_0, ...), custom_call_target="tpu_custom_call" | custom-call | tf_op jit(solution)/shard_map/lamb/pallas_call | solution.py:532

commit v3 on v2

--- a/solution.py
+++ b/solution.py
@@ -8,7 +8,7 @@
 
 TABLES = 26
 CAP = 8
-HEAD = 1
+HEAD = 0
 
 beta_one = 0.9
 beta_two = 0.999
@@ -263,7 +263,8 @@
 
     steps = tokens // chunk
     head = min(HEAD, steps)
-    lax.fori_loop(0, head, forward, 0)
+    if head:
+        lax.fori_loop(0, head, forward, 0)
     recv(e_plane)
     e_z = z_spread(0, e_recv)
     recv(t_plane)

time: 42.3 us -> 42.2 us (level)
  no operation moved by 1% of the time
where the time goes in v3:
time: 42.2 us; the launch traced here: 42 us
  Pallas kernels  41.4 us (98%)
  between operations  0.66 us (2%)
    pallas_call x1, Pallas kernels, body(): pl.pallas_call(functools.partial(exchange_kernel, grps, shards, chunk), o...  36.6 us
    pallas_call x1, Pallas kernels, body(): pl.pallas_call(lamb_kernel, out_shape=shapes, in_specs=[anywhere] * 17, o...  4.82 us

profile of v3, /device:TPU:0, one launch (start us, length us, event | category | flops | bytes accessed | tf_op | source)
XLA Modules:
  0.0 42.0 jit_solution(2672726875371179528)
XLA Ops:
  0.6 36.6 %tower_exchange.1 = (f32[1024,128]{1,0:T(8,128)}, f32[1024,128]{1,0:T(8,128)}, f32[16,512]{1,0:T(8,128)}, f32[512,256]{1,0:T(8,128)}, f32[256,128]{1,0:T(8,128)}) custom-call(s32[1,32]{1,0:T(1,128)} %touched.1, s32[1,1024]{1,0:T(1,128)} %bitcast.16, s32[1,128]{1,0:T(1,128)} %bitcast.17, bf16[256,128]{1,0:T(8,128)(2,1)} %bitcast.15, f32[13,512]{1,0:T(8,128)} %refs_8_.1, ...), custom_call_target="tpu_custom_call" | custom-call | tf_op jit(solution)/shard_map/tower_exchange/pallas_call | solution.py:461
  37.2 4.8 %lamb.1 = (f32[1024,128]{1,0:T(8,128)}, f32[1024,128]{1,0:T(8,128)}, f32[1024,128]{1,0:T(8,128)}, f32[13,512]{1,0:T(8,128)}, f32[512,256]{1,0:T(8,128)}, /*index...) custom-call(f32[1024,128]{1,0:T(8,128)} %get-tuple-element.29.refs_0, ...), custom_call_target="tpu_custom_call" | custom-call | tf_op jit(solution)/shard_map/lamb/pallas_call | solution.py:533
